TPU v7x, 32 devices: a whole 2x2x4 slice. The times are simulated.
32 devices in a mesh: clip: 8 (over y, x, core), tm: 4 (over z).
Axes of the slice: x: 2, y: 2, z: 4, core: 2. Of those that a mesh axis runs over, the one named last changes fastest.
Arguments:
- features: bfloat16 [16, 4, 64, 1024], P('clip', 'tm'), may hold values from -6 to 6
- flow_forward: int32 [16, 4, 2, 16], P('clip', 'tm'), may hold values from -4 to 4
- flow_backward: int32 [16, 4, 2, 16], P('clip', 'tm'), may hold values from -4 to 4
- w_forward_in: bfloat16 [64, 1152], replicated, may hold values from -0.1875 to 0.1875
- b_forward_in: float32 [64], replicated, may hold values from -3 to 3
- w_forward_out: bfloat16 [64, 576], replicated, may hold values from -0.25 to 0.25
- b_forward_out: float32 [64], replicated, may hold values from -3 to 3
- w_backward_in: bfloat16 [64, 1152], replicated, may hold values from -0.1875 to 0.1875
- b_backward_in: float32 [64], replicated, may hold values from -3 to 3
- w_backward_out: bfloat16 [64, 576], replicated, may hold values from -0.25 to 0.25
- b_backward_out: float32 [64], replicated, may hold values from -3 to 3
- w_merge: bfloat16 [64, 1152], replicated, may hold values from -0.1875 to 0.1875
- b_merge: float32 [64], replicated, may hold values from -3 to 3
- w_head: bfloat16 [48, 64], replicated, may hold values from -0.75 to 0.75
- b_head: float32 [48], replicated, may hold values from -3 to 3
- target: bfloat16 [16, 4, 48, 1024], P('clip', 'tm'), may hold values from -24 to 24
Outputs:
- restored: bfloat16 [16, 4, 48, 1024], P('clip', 'tm')
- grad_merge: float32 [64, 1152], replicated
- grad_head: float32 [48, 64], replicated
- loss: float32 [], replicated
All inputs are finite; a program needn't handle non-finite values.
Results may differ from a plain program's by a relative error of at most 0.0085.
Values may be sent and summed in bfloat16 or wider, within the bound.
A program may use at most 64 MiB of HBM per device.

v0:
```python
import jax
import jax.numpy as jnp
from jax import lax
from jax.sharding import PartitionSpec as P

CHANNELS = 64
SUBPIX = 48
PATCH_ROWS = 32
PATCH_COLS = 32
PIXELS = 1024


flow_reach = 4
tile_rows = 8
block_side = 8
clip_limit = 128.0
leak_slope = 0.1


def shifted(value, axis, steps):
    count = lax.axis_size(axis)
    first, last = (max(0, -steps), min(count, count - steps))
    return lax.ppermute(value, axis, [(source, source + steps) for source in range(first, last)])


def flat_taps(source, height, width):
    pixels = height * width
    padded = jnp.pad(source, ((0, 0), (width + 1, width + 1)))
    col_pos = lax.broadcasted_iota(jnp.int32, (1, pixels), 1) % width
    layers = []
    for row_off in (-1, 0, 1):
        for col_off in (-1, 0, 1):
            start = width + 1 + row_off * width + col_off
            piece = padded[:, start : start + pixels]
            if col_off != 0:
                valid = (col_pos + col_off >= 0) & (col_pos + col_off < width)
                piece = jnp.where(valid, piece, jnp.zeros_like(piece))
            layers.append(piece)
    return layers


def apply_taps(weight, groups):
    total_in = sum((group[0].shape[0] for group in groups))
    result = None
    for tap_index in range(9):
        offset = tap_index * total_in
        for group in groups:
            width_in = group[tap_index].shape[0]
            block = weight[:, offset : offset + width_in]
            term = jnp.dot(block, group[tap_index], preferred_element_type=jnp.float32)
            result = term if result is None else result + term
            offset = offset + width_in
    return result


def warp_state(hidden_state, flow_map, height, width):
    padded = jnp.pad(hidden_state, ((0, 0), (flow_reach * width, flow_reach * width)))
    grid_shape = (height // block_side, width // block_side)
    shift_rows = jnp.repeat(
        jnp.repeat(flow_map[0].reshape(grid_shape), block_side, 0), block_side, 1
    )
    shift_cols = jnp.repeat(
        jnp.repeat(flow_map[1].reshape(grid_shape), block_side, 0), block_side, 1
    )
    row_pos = lax.broadcasted_iota(jnp.int32, (height, width), 0)
    col_pos = lax.broadcasted_iota(jnp.int32, (height, width), 1)
    source_col = col_pos + shift_cols
    inside = (source_col >= 0) & (source_col < width)
    window_rows = tile_rows + 2 * flow_reach
    window_cell = lax.broadcasted_iota(jnp.int32, (window_rows * width, tile_rows * width), 0)
    pieces = []
    for tile_index in range(height // tile_rows):
        row_start = tile_index * tile_rows
        window = padded[:, row_start * width : (row_start + window_rows) * width]
        local_row = (
            row_pos[row_start : row_start + tile_rows]
            + shift_rows[row_start : row_start + tile_rows]
            - row_start
            + flow_reach
        )
        target_cell = local_row * width + source_col[row_start : row_start + tile_rows]
        target_cell = jnp.where(inside[row_start : row_start + tile_rows], target_cell, -1).reshape(
            -1
        )
        one_hot = (window_cell == target_cell[None, :]).astype(jnp.bfloat16)
        pieces.append(jnp.dot(window, one_hot, preferred_element_type=jnp.float32))
    return jnp.concatenate(pieces, axis=1).astype(jnp.bfloat16)


def propagate(prior_state, feature, flow_map, weights, height, width):
    w_first, b_first, w_second, b_second = weights
    warped = warp_state(prior_state, flow_map, height, width)
    first_out = (
        apply_taps(w_first, (flat_taps(warped, height, width), flat_taps(feature, height, width)))
        + b_first[:, None]
    )
    first_out = jax.nn.leaky_relu(first_out, leak_slope).astype(jnp.bfloat16)
    second_out = apply_taps(w_second, (flat_taps(first_out, height, width),)) + b_second[:, None]
    return (warped.astype(jnp.float32) + second_out).astype(jnp.bfloat16)


def merge_and_grade(fwd_state, bwd_state, target_frame, merge_weights, height, width, loss_scale):
    w_merge, b_merge, w_head, b_head = merge_weights
    groups = (flat_taps(fwd_state, height, width), flat_taps(bwd_state, height, width))
    mixed_pre = apply_taps(w_merge, groups) + b_merge[:, None]
    sigmoid_part = jax.nn.sigmoid(mixed_pre)
    active = (mixed_pre * sigmoid_part).astype(jnp.bfloat16)
    output = jnp.dot(w_head, active, preferred_element_type=jnp.float32) + b_head[:, None]
    misfit = output - target_frame.astype(jnp.float32)
    loss_part = 0.5 * loss_scale * jnp.sum(misfit * misfit)
    errors = (misfit * loss_scale).astype(jnp.bfloat16)
    grad_head = lax.dot_general(
        errors, active, (((1,), (1,)), ((), ())), preferred_element_type=jnp.float32
    )
    back_grad = lax.dot_general(
        w_head, errors, (((0,), (0,)), ((), ())), preferred_element_type=jnp.float32
    )
    silu_slope = sigmoid_part * (1.0 + mixed_pre * (1.0 - sigmoid_part))
    d_mixed = (back_grad * silu_slope).astype(jnp.bfloat16)
    blocks = []
    for tap_index in range(9):
        for group in groups:
            blocks.append(
                lax.dot_general(
                    d_mixed,
                    group[tap_index],
                    (((1,), (1,)), ((), ())),
                    preferred_element_type=jnp.float32,
                )
            )
    grad_merge = jnp.concatenate(blocks, axis=1)
    return (output.astype(jnp.bfloat16), grad_merge, grad_head, loss_part)


def on_device(
    features,
    flow_forward,
    flow_backward,
    w_forward_in,
    b_forward_in,
    w_forward_out,
    b_forward_out,
    w_backward_in,
    b_backward_in,
    w_backward_out,
    b_backward_out,
    w_merge,
    b_merge,
    w_head,
    b_head,
    target,
):
    fwd_weights = (w_forward_in, b_forward_in, w_forward_out, b_forward_out)
    bwd_weights = (w_backward_in, b_backward_in, w_backward_out, b_backward_out)
    merge_weights = (w_merge, b_merge, w_head, b_head)
    micro_clips = features.shape[0]
    sections = lax.axis_size("tm")
    section_index = lax.axis_index("tm")
    turns = micro_clips + sections - 1
    frame_feats = features[:, 0]
    fwd_flows = flow_forward[:, 0]
    bwd_flows = flow_backward[:, 0]
    blank_states = jnp.zeros((micro_clips, CHANNELS, PIXELS), jnp.bfloat16)
    seed_state = jnp.zeros((CHANNELS, PIXELS), jnp.bfloat16)
    bwd_offset = sections - 1 - section_index

    def advance(turn_index, offset, incoming, states, flows, weights):
        member = turn_index - offset
        active_flag = (member >= 0) & (member < micro_clips)
        member = jnp.clip(member, 0, micro_clips - 1)
        feature = lax.dynamic_index_in_dim(frame_feats, member, 0, keepdims=False)
        flow_map = lax.dynamic_index_in_dim(flows, member, 0, keepdims=False)
        produced = propagate(incoming, feature, flow_map, weights, PATCH_ROWS, PATCH_COLS)
        former = lax.dynamic_index_in_dim(states, member, 0, keepdims=False)
        states = lax.dynamic_update_index_in_dim(
            states, jnp.where(active_flag, produced, former), member, 0
        )
        return (produced, states)

    def forward_turn(turn_index, carried):
        produced, states = advance(
            turn_index, section_index, carried[0], carried[1], fwd_flows, fwd_weights
        )
        return (shifted(produced, "tm", 1), states)

    def backward_turn(turn_index, carried):
        produced, states = advance(
            turn_index, bwd_offset, carried[0], carried[1], bwd_flows, bwd_weights
        )
        return (shifted(produced, "tm", -1), states)

    fwd_states = lax.fori_loop(0, turns, forward_turn, (seed_state, blank_states))[1]
    bwd_states = lax.fori_loop(0, turns, backward_turn, (seed_state, blank_states))[1]
    loss_scale = 1.0 / (micro_clips * lax.axis_size("clip") * sections)

    def grade_member(totals, inputs):
        frame_out, grad_merge, grad_head, loss_part = merge_and_grade(
            inputs[0], inputs[1], inputs[2], merge_weights, PATCH_ROWS, PATCH_COLS, loss_scale
        )
        return ((totals[0] + grad_merge, totals[1] + grad_head, totals[2] + loss_part), frame_out)

    initial = (
        jnp.zeros((CHANNELS, 18 * CHANNELS), jnp.float32),
        jnp.zeros((SUBPIX, CHANNELS), jnp.float32),
        jnp.zeros((), jnp.float32),
    )
    totals, frames_out = lax.scan(grade_member, initial, (fwd_states, bwd_states, target[:, 0]))
    restored = frames_out[:, None]
    grad_merge, grad_head, loss_total = lax.psum((totals[0], totals[1], totals[2]), ("clip", "tm"))
    squares = jnp.sum(grad_merge * grad_merge) + jnp.sum(grad_head * grad_head)
    factor = jnp.minimum(1.0, clip_limit / jnp.sqrt(squares + 1e-06))
    return (restored, grad_merge * factor, grad_head * factor, loss_total)


def solution(mesh):
    in_specs = (
        P("clip", "tm", None, None),
        P("clip", "tm", None, None),
        P("clip", "tm", None, None),
        P(),
        P(),
        P(),
        P(),
        P(),
        P(),
        P(),
        P(),
        P(),
        P(),
        P(),
        P(),
        P("clip", "tm", None, None),
    )
    out_specs = (P("clip", "tm", None, None), P(), P(), P())
    return jax.shard_map(
        on_device, mesh=mesh, in_specs=in_specs, out_specs=out_specs, check_vma=False
    )
```

profile of v0, /device:TPU:0, one launch (start us, length us, event | category | flops | bytes accessed | tf_op | source)
XLA Modules:
  0.0 339.3 jit_solution(3447712072973825057)
XLA Ops:
  7.4 0.8 copy-done.4
  8.2 86.1 %while.57 = (s32[]{:T(128)}, bf16[64,1024]{1,0:T(8,128)(2,1)S(1)}, bf16[2,64,1024]{2,1,0:T(8,128)(2,1)S(1)}, s32[]{:T(128)}, s32[2,2,16]{2,1,0:T(2,128)S(1)}, /*...) while((s32[]{:T(128)}, bf16[64,1024]{1,0:T(8,128)(2,1)S(1)}, ...), condition=%wide.region_1.2_spmd, body=%wide.region_0.1_spmd.sunk | while | flops 299203584 | bytes 19935880 | solution.py:192
  15.3 0.3 fusion.830
  15.6 0.6 copy-done.5
  18.1 0.3 bitcast_dynamic-update-slice_fusion.6
  18.4 4.9 %collective-permute-start = (bf16[64,1024]{1,0:T(8,128)(2,1)S(1)}, bf16[64,1024]{1,0:T(8,128)(2,1)S(1)}, u32[]{:S(2)}, u32[]{:S(2)}) collective-permute-start(bf16[64,1024]{1,0:T(8,128)(2,1)S(1)} %get-tuple-element.1151), channel_id=1, source_target_pairs={{0,1},{1,2},{2,3},{4,5},{5,6},{6,7},{8,9},{9,10},{10,11},{12,13},{... | collective-permute-start | bytes 393224 | tf_op jit(solution)/shard_map/while/body/eval_jaxpr/ppermute | solution.py:23
  23.4 2.7 collective-permute-done
  33.2 0.3 fusion.830
  33.4 0.6 copy-done.5
  36.0 0.3 bitcast_dynamic-update-slice_fusion.6
  36.3 4.4 %collective-permute-start = (bf16[64,1024]{1,0:T(8,128)(2,1)S(1)}, bf16[64,1024]{1,0:T(8,128)(2,1)S(1)}, u32[]{:S(2)}, u32[]{:S(2)}) collective-permute-start(bf16[64,1024]{1,0:T(8,128)(2,1)S(1)} %get-tuple-element.1151), channel_id=1, source_target_pairs={{0,1},{1,2},{2,3},{4,5},{5,6},{6,7},{8,9},{9,10},{10,11},{12,13},{... | collective-permute-start | bytes 393224 | tf_op jit(solution)/shard_map/while/body/eval_jaxpr/ppermute | solution.py:23
  40.7 2.5 collective-permute-done
  50.2 0.3 fusion.830
  50.5 0.6 copy-done.5
  53.1 0.3 bitcast_dynamic-update-slice_fusion.6
  53.3 4.4 %collective-permute-start = (bf16[64,1024]{1,0:T(8,128)(2,1)S(1)}, bf16[64,1024]{1,0:T(8,128)(2,1)S(1)}, u32[]{:S(2)}, u32[]{:S(2)}) collective-permute-start(bf16[64,1024]{1,0:T(8,128)(2,1)S(1)} %get-tuple-element.1151), channel_id=1, source_target_pairs={{0,1},{1,2},{2,3},{4,5},{5,6},{6,7},{8,9},{9,10},{10,11},{12,13},{... | collective-permute-start | bytes 393224 | tf_op jit(solution)/shard_map/while/body/eval_jaxpr/ppermute | solution.py:23
  57.7 2.5 collective-permute-done
  67.3 0.3 fusion.830
  67.5 0.6 copy-done.5
  70.1 0.3 bitcast_dynamic-update-slice_fusion.6
  70.4 4.4 %collective-permute-start = (bf16[64,1024]{1,0:T(8,128)(2,1)S(1)}, bf16[64,1024]{1,0:T(8,128)(2,1)S(1)}, u32[]{:S(2)}, u32[]{:S(2)}) collective-permute-start(bf16[64,1024]{1,0:T(8,128)(2,1)S(1)} %get-tuple-element.1151), channel_id=1, source_target_pairs={{0,1},{1,2},{2,3},{4,5},{5,6},{6,7},{8,9},{9,10},{10,11},{12,13},{... | collective-permute-start | bytes 393224 | tf_op jit(solution)/shard_map/while/body/eval_jaxpr/ppermute | solution.py:23
  74.7 2.5 collective-permute-done
  84.3 0.3 fusion.830
  84.6 0.6 copy-done.5
  87.1 0.3 bitcast_dynamic-update-slice_fusion.6
  87.4 4.4 %collective-permute-start = (bf16[64,1024]{1,0:T(8,128)(2,1)S(1)}, bf16[64,1024]{1,0:T(8,128)(2,1)S(1)}, u32[]{:S(2)}, u32[]{:S(2)}) collective-permute-start(bf16[64,1024]{1,0:T(8,128)(2,1)S(1)} %get-tuple-element.1151), channel_id=1, source_target_pairs={{0,1},{1,2},{2,3},{4,5},{5,6},{6,7},{8,9},{9,10},{10,11},{12,13},{... | collective-permute-start | bytes 393224 | tf_op jit(solution)/shard_map/while/body/eval_jaxpr/ppermute | solution.py:23
  91.8 2.5 collective-permute-done
  94.4 0.8 copy-done.1
  95.3 82.6 %while.58 = (s32[]{:T(128)}, bf16[64,1024]{1,0:T(8,128)(2,1)S(1)}, bf16[2,64,1024]{2,1,0:T(8,128)(2,1)S(1)}, s32[]{:T(128)}, s32[2,2,16]{2,1,0:T(2,128)S(1)}, /*...) while((s32[]{:T(128)}, bf16[64,1024]{1,0:T(8,128)(2,1)S(1)}, ...), condition=%wide.region_3.4_spmd, body=%wide.region_2.3_spmd.sunk | while | flops 299203584 | bytes 19640940 | solution.py:193
  102.4 0.3 fusion.891
  104.6 0.3 bitcast_dynamic-update-slice_fusion.7
  104.9 1.3 collective-permute-start.1
  106.2 6.0 %collective-permute-done.1 = bf16[64,1024]{1,0:T(8,128)(2,1)S(1)} collective-permute-done((bf16[64,1024]{1,0:T(8,128)(2,1)S(1)}, bf16[64,1024]{1,0:T(8,128)(2,1)S(1)}, u32[]{:S(2)}, u32[]{:S(2)}) %collective-permute-start.1) | collective-permute-done | bytes 131104 | tf_op jit(solution)/shard_map/while/body/eval_jaxpr/ppermute | solution.py:23
  119.2 0.3 fusion.891
  121.5 0.3 bitcast_dynamic-update-slice_fusion.7
  121.7 1.3 collective-permute-start.1
  123.1 5.6 %collective-permute-done.1 = bf16[64,1024]{1,0:T(8,128)(2,1)S(1)} collective-permute-done((bf16[64,1024]{1,0:T(8,128)(2,1)S(1)}, bf16[64,1024]{1,0:T(8,128)(2,1)S(1)}, u32[]{:S(2)}, u32[]{:S(2)}) %collective-permute-start.1) | collective-permute-done | bytes 131104 | tf_op jit(solution)/shard_map/while/body/eval_jaxpr/ppermute | solution.py:23
  135.7 0.3 fusion.891
  137.9 0.3 bitcast_dynamic-update-slice_fusion.7
  138.2 1.3 collective-permute-start.1
  139.5 5.6 %collective-permute-done.1 = bf16[64,1024]{1,0:T(8,128)(2,1)S(1)} collective-permute-done((bf16[64,1024]{1,0:T(8,128)(2,1)S(1)}, bf16[64,1024]{1,0:T(8,128)(2,1)S(1)}, u32[]{:S(2)}, u32[]{:S(2)}) %collective-permute-start.1) | collective-permute-done | bytes 131104 | tf_op jit(solution)/shard_map/while/body/eval_jaxpr/ppermute | solution.py:23
  152.1 0.3 fusion.891
  154.3 0.3 bitcast_dynamic-update-slice_fusion.7
  154.6 1.3 collective-permute-start.1
  155.9 5.6 %collective-permute-done.1 = bf16[64,1024]{1,0:T(8,128)(2,1)S(1)} collective-permute-done((bf16[64,1024]{1,0:T(8,128)(2,1)S(1)}, bf16[64,1024]{1,0:T(8,128)(2,1)S(1)}, u32[]{:S(2)}, u32[]{:S(2)}) %collective-permute-start.1) | collective-permute-done | bytes 131104 | tf_op jit(solution)/shard_map/while/body/eval_jaxpr/ppermute | solution.py:23
  168.5 0.3 fusion.891
  170.7 0.3 bitcast_dynamic-update-slice_fusion.7
  171.0 1.3 collective-permute-start.1
  172.3 5.6 %collective-permute-done.1 = bf16[64,1024]{1,0:T(8,128)(2,1)S(1)} collective-permute-done((bf16[64,1024]{1,0:T(8,128)(2,1)S(1)}, bf16[64,1024]{1,0:T(8,128)(2,1)S(1)}, u32[]{:S(2)}, u32[]{:S(2)}) %collective-permute-start.1) | collective-permute-done | bytes 131104 | tf_op jit(solution)/shard_map/while/body/eval_jaxpr/ppermute | solution.py:23
  177.9 0.6 copy-done.10
  178.5 22.3 %while.59 = (s32[]{:T(128)}, f32[64,1152]{1,0:T(8,128)S(1)}, f32[48,64]{1,0:T(8,128)S(1)}, f32[]{:T(128)}, bf16[2,48,1024]{2,1,0:T(8,128)(2,1)S(1)}, /*index=5*/...) while((s32[]{:T(128)}, f32[64,1152]{1,0:T(8,128)S(1)}, ...), condition=%wide.region_6.7_spmd.clone, body=%wide.region_4.6_spmd.clone.sunk | while | flops 325101568 | bytes 20380548 | solution.py:207
  182.8 0.3 multiply_convert_fusion.3
  183.1 0.8 multiply_reduce_fusion.4
  191.8 0.3 convolution_add_fusion.176
  192.7 0.3 convolution_add_fusion.180
  194.0 0.3 multiply_convert_fusion.3
  194.3 0.8 multiply_reduce_fusion.4
  200.9 0.7 copy-done.3
  201.6 42.1 %all-reduce.10 = (f32[48,64]{1,0:T(8,128)S(1)}, f32[]{:T(128)}) all-reduce(f32[48,64]{1,0:T(8,128)S(1)} %get-tuple-element.806, f32[]{:T(128)} %get-tuple-element.807), channel_id=1, replica_groups=mesh['clip'=8,'tm'=4] {'clip','tm'}, use_global_device_ids=true, to_apply=%region_9.10 | all-reduce | flops 3073 | bytes 24584 | tf_op jit(solution)/shard_map/psum | solution.py:209
  243.8 0.6 multiply_reduce_fusion.2
  244.4 83.7 %all-reduce.13.cloned.1.call-done = f32[64,1152]{1,0:T(8,128)} async-done(((f32[64,1152]{1,0:T(8,128)}), f32[64,1152]{1,0:T(8,128)}) %all-reduce.13.cloned.1.call-update) | async-done | bytes 294928 | tf_op jit(solution)/shard_map/psum | solution.py:209
  328.1 1.7 multiply_reduce_fusion.1
  331.1 0.6 broadcast_multiply_fusion.1
  331.7 0.7 broadcast_multiply_fusion
  (730 shorter events, 105.6 us)
Async XLA Ops:
  7.2 1.0 copy-start.4
  7.2 320.9 %all-reduce.13.cloned.1.call-start = ((), (), s32[]{:S(2)}) async-start(), calls=%async_computation | async-start | bytes 589824 | tf_op jit(solution)/shard_map/psum | solution.py:209
  7.3 0.9 copy-start
  7.3 0.9 copy-start.11
  7.3 0.9 copy-start.13
  7.3 0.9 copy-start.16
  15.3 0.9 copy-start.5
  18.4 7.7 %collective-permute-start = (bf16[64,1024]{1,0:T(8,128)(2,1)S(1)}, bf16[64,1024]{1,0:T(8,128)(2,1)S(1)}, u32[]{:S(2)}, u32[]{:S(2)}) collective-permute-start(bf16[64,1024]{1,0:T(8,128)(2,1)S(1)} %get-tuple-element.1151), channel_id=1, source_target_pairs={{0,1},{1,2},{2,3},{4,5},{5,6},{6,7},{8,9},{9,10},{10,11},{12,13},{... | collective-permute-start | bytes 393224 | tf_op jit(solution)/shard_map/while/body/eval_jaxpr/ppermute | solution.py:23
  33.1 0.9 copy-start.5
  36.3 6.9 %collective-permute-start = (bf16[64,1024]{1,0:T(8,128)(2,1)S(1)}, bf16[64,1024]{1,0:T(8,128)(2,1)S(1)}, u32[]{:S(2)}, u32[]{:S(2)}) collective-permute-start(bf16[64,1024]{1,0:T(8,128)(2,1)S(1)} %get-tuple-element.1151), channel_id=1, source_target_pairs={{0,1},{1,2},{2,3},{4,5},{5,6},{6,7},{8,9},{9,10},{10,11},{12,13},{... | collective-permute-start | bytes 393224 | tf_op jit(solution)/shard_map/while/body/eval_jaxpr/ppermute | solution.py:23
  50.2 0.9 copy-start.5
  53.3 6.9 %collective-permute-start = (bf16[64,1024]{1,0:T(8,128)(2,1)S(1)}, bf16[64,1024]{1,0:T(8,128)(2,1)S(1)}, u32[]{:S(2)}, u32[]{:S(2)}) collective-permute-start(bf16[64,1024]{1,0:T(8,128)(2,1)S(1)} %get-tuple-element.1151), channel_id=1, source_target_pairs={{0,1},{1,2},{2,3},{4,5},{5,6},{6,7},{8,9},{9,10},{10,11},{12,13},{... | collective-permute-start | bytes 393224 | tf_op jit(solution)/shard_map/while/body/eval_jaxpr/ppermute | solution.py:23
  67.2 0.9 copy-start.5
  70.4 6.9 %collective-permute-start = (bf16[64,1024]{1,0:T(8,128)(2,1)S(1)}, bf16[64,1024]{1,0:T(8,128)(2,1)S(1)}, u32[]{:S(2)}, u32[]{:S(2)}) collective-permute-start(bf16[64,1024]{1,0:T(8,128)(2,1)S(1)} %get-tuple-element.1151), channel_id=1, source_target_pairs={{0,1},{1,2},{2,3},{4,5},{5,6},{6,7},{8,9},{9,10},{10,11},{12,13},{... | collective-permute-start | bytes 393224 | tf_op jit(solution)/shard_map/while/body/eval_jaxpr/ppermute | solution.py:23
  84.3 0.9 copy-start.5
  87.4 6.9 %collective-permute-start = (bf16[64,1024]{1,0:T(8,128)(2,1)S(1)}, bf16[64,1024]{1,0:T(8,128)(2,1)S(1)}, u32[]{:S(2)}, u32[]{:S(2)}) collective-permute-start(bf16[64,1024]{1,0:T(8,128)(2,1)S(1)} %get-tuple-element.1151), channel_id=1, source_target_pairs={{0,1},{1,2},{2,3},{4,5},{5,6},{6,7},{8,9},{9,10},{10,11},{12,13},{... | collective-permute-start | bytes 393224 | tf_op jit(solution)/shard_map/while/body/eval_jaxpr/ppermute | solution.py:23
  94.3 0.9 copy-start.1
  94.3 1.0 copy-start.6
  94.3 0.9 copy-start.12
  94.3 0.9 copy-start.14
  94.3 0.9 copy-start.17
  95.3 82.6 %copy-start.2 = (bf16[64,1152]{1,0:T(8,128)(2,1)S(1)}, bf16[64,1152]{1,0:T(8,128)(2,1)}, u32[]{:S(2)}) copy-start(bf16[64,1152]{1,0:T(8,128)(2,1)} %param.33) | copy-start | bytes 442372
  95.3 82.6 %copy-start.7 = (bf16[2,1,48,1024]{3,2,1,0:T(8,128)(2,1)S(1)}, bf16[2,1,48,1024]{3,2,1,0:T(8,128)(2,1)}, u32[]{:S(2)}) copy-start(bf16[2,1,48,1024]{3,2,1,0:T(8,128)(2,1)} %param.37) | copy-start | bytes 589828
  95.3 82.6 %copy-start.9 = (bf16[48,64]{1,0:T(8,128)(2,1)S(1)}, bf16[48,64]{1,0:T(8,128)(2,1)}, u32[]{:S(2)}) copy-start(bf16[48,64]{1,0:T(8,128)(2,1)} %param.35) | copy-start | bytes 18436
  104.9 7.3 %collective-permute-start.1 = (bf16[64,1024]{1,0:T(8,128)(2,1)S(1)}, bf16[64,1024]{1,0:T(8,128)(2,1)S(1)}, u32[]{:S(2)}, u32[]{:S(2)}) collective-permute-start(bf16[64,1024]{1,0:T(8,128)(2,1)S(1)} %get-tuple-element.1171), channel_id=1, source_target_pairs={{1,0},{2,1},{3,2},{5,4},{6,5},{7,6},{9,8},{10,9},{11,10},{13,12},{... | collective-permute-start | bytes 393224 | tf_op jit(solution)/shard_map/while/body/eval_jaxpr/ppermute | solution.py:23
  121.7 6.9 %collective-permute-start.1 = (bf16[64,1024]{1,0:T(8,128)(2,1)S(1)}, bf16[64,1024]{1,0:T(8,128)(2,1)S(1)}, u32[]{:S(2)}, u32[]{:S(2)}) collective-permute-start(bf16[64,1024]{1,0:T(8,128)(2,1)S(1)} %get-tuple-element.1171), channel_id=1, source_target_pairs={{1,0},{2,1},{3,2},{5,4},{6,5},{7,6},{9,8},{10,9},{11,10},{13,12},{... | collective-permute-start | bytes 393224 | tf_op jit(solution)/shard_map/while/body/eval_jaxpr/ppermute | solution.py:23
  138.2 6.9 %collective-permute-start.1 = (bf16[64,1024]{1,0:T(8,128)(2,1)S(1)}, bf16[64,1024]{1,0:T(8,128)(2,1)S(1)}, u32[]{:S(2)}, u32[]{:S(2)}) collective-permute-start(bf16[64,1024]{1,0:T(8,128)(2,1)S(1)} %get-tuple-element.1171), channel_id=1, source_target_pairs={{1,0},{2,1},{3,2},{5,4},{6,5},{7,6},{9,8},{10,9},{11,10},{13,12},{... | collective-permute-start | bytes 393224 | tf_op jit(solution)/shard_map/while/body/eval_jaxpr/ppermute | solution.py:23
  154.6 6.9 %collective-permute-start.1 = (bf16[64,1024]{1,0:T(8,128)(2,1)S(1)}, bf16[64,1024]{1,0:T(8,128)(2,1)S(1)}, u32[]{:S(2)}, u32[]{:S(2)}) collective-permute-start(bf16[64,1024]{1,0:T(8,128)(2,1)S(1)} %get-tuple-element.1171), channel_id=1, source_target_pairs={{1,0},{2,1},{3,2},{5,4},{6,5},{7,6},{9,8},{10,9},{11,10},{13,12},{... | collective-permute-start | bytes 393224 | tf_op jit(solution)/shard_map/while/body/eval_jaxpr/ppermute | solution.py:23
  171.0 6.9 %collective-permute-start.1 = (bf16[64,1024]{1,0:T(8,128)(2,1)S(1)}, bf16[64,1024]{1,0:T(8,128)(2,1)S(1)}, u32[]{:S(2)}, u32[]{:S(2)}) collective-permute-start(bf16[64,1024]{1,0:T(8,128)(2,1)S(1)} %get-tuple-element.1171), channel_id=1, source_target_pairs={{1,0},{2,1},{3,2},{5,4},{6,5},{7,6},{9,8},{10,9},{11,10},{13,12},{... | collective-permute-start | bytes 393224 | tf_op jit(solution)/shard_map/while/body/eval_jaxpr/ppermute | solution.py:23
  177.9 0.7 copy-start.10
  177.9 0.7 copy-start.18
  200.9 0.7 copy-start.3
  200.9 128.9 %copy-start.15 = (bf16[2,48,1024]{2,1,0:T(8,128)(2,1)}, bf16[2,48,1024]{2,1,0:T(8,128)(2,1)S(1)}, u32[]{:S(2)}) copy-start(bf16[2,48,1024]{2,1,0:T(8,128)(2,1)S(1)} %get-tuple-element.804) | copy-start | bytes 589828
  328.1 3.6 %copy-start.8 = (f32[64,1152]{1,0:T(8,128)S(1)}, f32[64,1152]{1,0:T(8,128)}, u32[]{:S(2)}) copy-start(f32[64,1152]{1,0:T(8,128)} %all-reduce.13.cloned.1.call-done) | copy-start | bytes 884740
Sparse Core Ops, SparseCore 0:
  201.8 126.2 all-reduce.12
where the time goes:
time: 340 us; the launch traced here: 339 us
  waiting for transfers between devices  125 us (37%)
  matrix products  94.5 us (28%)
  blocking collectives  42.1 us (12%)
  starting transfers between devices  28.9 us (8%)
  local copies, waits for them, and re-layouts  23.4 us (7%)
  between operations  15.5 us (5%)
  other arithmetic  5.51 us (2%)
  loops' own time  4.8 us (1%)
    psum x1, waiting for transfers between devices, on_device(): lax.psum((totals[0], totals[1], totals[2]), ('clip', 'tm'))  83.7 us
    dot_general x306, matrix products, apply_taps(): term = jnp.dot(block, group[tap_index], preferred_element_type=jnp.float32)  74.1 us
    psum x1, blocking collectives, on_device(): lax.psum((totals[0], totals[1], totals[2]), ('clip', 'tm'))  42.1 us
    ppermute x10, waiting for transfers between devices, shifted(): lax.ppermute(value, axis, [(source, source + steps) for source in range(f...  40.9 us
    ppermute x10, starting transfers between devices, shifted(): lax.ppermute(value, axis, [(source, source + steps) for source in range(f...  28.9 us
    dot_general x40, matrix products, warp_state(): pieces.append(jnp.dot(window, one_hot, preferred_element_type=jnp.float32))  9.39 us
    dot_general x36, matrix products, merge_and_grade(): lax.dot_general(d_mixed, group[tap_index], (((1,), (1,)), ((), ())), pref...  8.63 us
  transfers between devices with their start and end apart: 11, of which 11 were waited for; matrix products, arithmetic and copies ran while one was open for 0% of the time, Pallas kernels for 0%

commit v1 on v0

v1 whole, which is shorter than its diff:
```python
import functools

import jax
import jax.numpy as jnp
from jax import lax
from jax.experimental import pallas as pl
from jax.experimental.pallas import tpu as pltpu
from jax.sharding import PartitionSpec as P

CHANNELS = 64
SUBPIX = 48
WIDTH = 32
PIXELS = 1024
BLOCK = 8
REACH = 4
TILE = 256
MARGIN = REACH * WIDTH
WINDOW = TILE + 2 * MARGIN
CLIP_LIMIT = 128.0
LEAK = 0.1
PACK_ROWS = 256
PACK_COLS = 384
MESH = pl.DeviceIdType.MESH
BF = jnp.bfloat16
F32 = jnp.float32


def roll_lanes(value, shift):
    return pltpu.roll(value, shift % PIXELS, 1)


def lane_masks():
    lane = lax.broadcasted_iota(jnp.int32, (1, PIXELS), 1)
    col = lane % WIDTH
    return (
        (col != 0),
        (col != WIDTH - 1),
        (lane >= WIDTH),
        (lane < PIXELS - WIDTH),
    )


def column_taps(value, masks):
    left = jnp.where(masks[0], roll_lanes(value, 1), 0.0)
    right = jnp.where(masks[1], roll_lanes(value, -1), 0.0)
    return [left.astype(BF), value.astype(BF), right.astype(BF)]


def row_sum(stacked, masks):
    up = jnp.where(masks[2], roll_lanes(stacked[:CHANNELS], WIDTH), 0.0)
    down = jnp.where(masks[3], roll_lanes(stacked[2 * CHANNELS :], -WIDTH), 0.0)
    return up + stacked[CHANNELS : 2 * CHANNELS] + down


def dot(a, b):
    return jnp.dot(a, b, preferred_element_type=F32)


def dot_t(a, b):
    return lax.dot_general(a, b, (((1,), (1,)), ((), ())), preferred_element_type=F32)


def stack_rows(weight):
    third = weight.shape[1] // 3
    return jnp.concatenate([weight[:, i * third : (i + 1) * third] for i in range(3)], axis=0)


def propagate(state, cells, feature, w_in, b_in, w_out, b_out, masks):
    window_cell = lax.broadcasted_iota(jnp.int32, (WINDOW, TILE), 0)
    pieces = []
    for start in range(0, PIXELS, TILE):
        one_hot = (window_cell == cells[:, start : start + TILE]).astype(F32).astype(BF)
        pieces.append(dot(state[:, start : start + WINDOW], one_hot))
    warped = jnp.concatenate(pieces, axis=1)
    taps_g = column_taps(warped, masks)
    taps_x = column_taps(feature.astype(F32), masks)
    joined = jnp.concatenate([t for pair in zip(taps_g, taps_x) for t in pair], axis=0)
    hidden = row_sum(dot(w_in, joined), masks) + b_in
    hidden = jnp.where(hidden >= 0, hidden, LEAK * hidden).astype(BF).astype(F32)
    taps_a = jnp.concatenate(column_taps(hidden, masks), axis=0)
    update = row_sum(dot(w_out, taps_a), masks) + b_out
    return (warped + update).astype(BF)


def merge(hf, hb, target, w_merge, b_merge, w_head, b_head, scale, masks):
    taps_f = column_taps(hf.astype(F32), masks)
    taps_b = column_taps(hb.astype(F32), masks)
    joined = jnp.concatenate([t for pair in zip(taps_f, taps_b) for t in pair], axis=0)
    m = row_sum(dot(w_merge, joined), masks) + b_merge
    sig = jax.nn.sigmoid(m)
    active = (m * sig).astype(BF)
    out = dot(w_head, active) + b_head
    misfit = out - target.astype(F32)
    loss = jnp.sum(misfit * misfit, axis=0, keepdims=True)
    loss = jnp.sum(loss, axis=1, keepdims=True) * (0.5 * scale)
    err = (misfit * scale).astype(BF)
    g_head = dot_t(err, active)
    back = lax.dot_general(w_head, err, (((0,), (0,)), ((), ())), preferred_element_type=F32)
    d_m = (back * (sig * (1.0 + m * (1.0 - sig)))).astype(BF).astype(F32)
    above = jnp.where(masks[3], roll_lanes(d_m, -WIDTH), 0.0).astype(BF)
    below = jnp.where(masks[2], roll_lanes(d_m, WIDTH), 0.0).astype(BF)
    g_merge = dot_t(jnp.concatenate([above, d_m.astype(BF), below], axis=0), joined)
    return out.astype(BF), g_merge, g_head, loss


def gather_kernel(sections, feat_ref, cell_ref, feat_out, cell_out, local_sem, send_sem, recv_sem):
    me = lax.axis_index("tm")
    barrier = pltpu.get_barrier_semaphore()
    for off in range(1, sections):
        pl.semaphore_signal(
            barrier, 1, device_id={"tm": lax.rem(me + off, sections)}, device_id_type=MESH
        )
    pl.semaphore_wait(barrier, sections - 1)
    copies = []
    for k, (src, dst) in enumerate(((cell_ref, cell_out), (feat_ref, feat_out))):
        for off in range(1, sections):
            copies.append(
                pltpu.make_async_remote_copy(
                    src,
                    dst.at[me],
                    send_sem.at[k, off],
                    recv_sem.at[k, off],
                    device_id={"tm": lax.rem(me + off, sections)},
                    device_id_type=MESH,
                )
            )
        copies.append(pltpu.make_async_copy(src, dst.at[me], local_sem.at[k]))
    for copy in copies:
        copy.start()
    for copy in copies:
        copy.wait()


def compute_kernel(
    sections,
    scale,
    feat_ref,
    cell_ref,
    wfi,
    bfi,
    wfo,
    bfo,
    wbi,
    bbi,
    wbo,
    bbo,
    wm,
    bm,
    wh,
    bh,
    target,
    out_ref,
    pack_ref,
    state,
    w_in,
    b_in,
    w_out,
    b_out,
):
    clips = target.shape[0]
    me = lax.axis_index("tm")
    masks = lane_masks()
    state[...] = jnp.zeros_like(state)
    for d, (wi, bi, wo, bo) in enumerate(((wfi, bfi, wfo, bfo), (wbi, bbi, wbo, bbo))):
        w_in[d] = stack_rows(wi[...])
        w_out[d] = stack_rows(wo[...])
        b_in[d] = bi[...]
        b_out[d] = bo[...]

    def turn(i, carry):
        forward = i <= me
        d = jnp.where(forward, 0, 1)
        frame = jnp.where(forward, i, sections + me - i)
        made = [
            propagate(
                state.at[d, c],
                cell_ref[frame, pl.ds(d * clips + c, 1), :],
                feat_ref[frame, c],
                w_in[d],
                b_in[d],
                w_out[d],
                b_out[d],
                masks,
            )
            for c in range(clips)
        ]
        for c in range(clips):
            state[d, c, :, MARGIN : MARGIN + PIXELS] = made[c]
        return carry

    lax.fori_loop(0, sections + 1, turn, 0)
    w_merge = stack_rows(wm[...])
    total = None
    for c in range(clips):
        inner = slice(MARGIN, MARGIN + PIXELS)
        out, *grads = merge(
            state[0, c, :, inner],
            state[1, c, :, inner],
            target[c],
            w_merge,
            bm[...],
            wh[...],
            bh[...],
            scale,
            masks,
        )
        out_ref[c] = out
        total = grads if total is None else [a + b for a, b in zip(total, grads)]
    rows = 3 * CHANNELS
    pack_ref[rows:, :] = jnp.zeros((PACK_ROWS - rows, PACK_COLS), F32)
    pack_ref[:rows, :] = total[0]
    pack_ref[rows : rows + SUBPIX, :CHANNELS] = total[1]
    pack_ref[rows + SUBPIX :, 128:256] = jnp.broadcast_to(
        total[2], (PACK_ROWS - rows - SUBPIX, 128)
    )


def reduce_kernel(
    group,
    sections,
    x_ref,
    gm_ref,
    gh_ref,
    loss_ref,
    got,
    part,
    full,
    send1,
    recv1,
    send2,
    recv2,
    send3,
    recv3,
):
    rows = PACK_ROWS // group
    me = lax.axis_index("clip")
    sec = lax.axis_index("tm")
    barrier = pltpu.get_barrier_semaphore()
    for off in range(1, group):
        pl.semaphore_signal(
            barrier, 1, device_id={"clip": lax.rem(me + off, group)}, device_id_type=MESH
        )
    for off in range(1, sections):
        pl.semaphore_signal(
            barrier, 1, device_id={"tm": lax.rem(sec + off, sections)}, device_id_type=MESH
        )
    pl.semaphore_wait(barrier, group + sections - 2)

    def chunk(i):
        return pl.ds(pl.multiple_of(i * rows, rows), rows)

    copies = []
    for off in range(1, group):
        peer = lax.rem(me + off, group)
        copies.append(
            pltpu.make_async_remote_copy(
                x_ref.at[chunk(peer)],
                got.at[off],
                send1.at[off],
                recv1.at[off],
                device_id={"clip": peer},
                device_id_type=MESH,
            )
        )
    for copy in copies:
        copy.start()
    total = x_ref[chunk(me)]
    for off, copy in enumerate(copies, 1):
        copy.wait()
        total = total + got[off]
    part[sec] = total
    copies = []
    for off in range(1, sections):
        copies.append(
            pltpu.make_async_remote_copy(
                part.at[sec],
                part.at[sec],
                send2.at[off],
                recv2.at[off],
                device_id={"tm": lax.rem(sec + off, sections)},
                device_id_type=MESH,
            )
        )
    for copy in copies:
        copy.start()
    for copy in copies:
        copy.wait()
    total = part[0]
    for s in range(1, sections):
        total = total + part[s]
    full[chunk(me)] = total
    copies = []
    for off in range(1, group):
        copies.append(
            pltpu.make_async_remote_copy(
                full.at[chunk(me)],
                full.at[chunk(me)],
                send3.at[off],
                recv3.at[off],
                device_id={"clip": lax.rem(me + off, group)},
                device_id_type=MESH,
            )
        )
    for copy in copies:
        copy.start()
    for copy in copies:
        copy.wait()
    top = 3 * CHANNELS
    g_merge = full[:top, :]
    g_head = full[top : top + SUBPIX, :CHANNELS]

    def squares(v):
        return jnp.sum(jnp.sum(v * v, axis=0, keepdims=True), axis=1, keepdims=True)

    factor = jnp.minimum(1.0, CLIP_LIMIT / jnp.sqrt(squares(g_merge) + squares(g_head) + 1e-06))
    for i in range(3):
        gm_ref[:, i * PACK_COLS : (i + 1) * PACK_COLS] = (
            g_merge[i * CHANNELS : (i + 1) * CHANNELS] * factor
        )
    gh_ref[...] = g_head * factor
    loss_ref[...] = full[top + SUBPIX : top + SUBPIX + 1, 128:129]


def window_cells(flow):
    side = WIDTH // BLOCK
    grid = flow.reshape(flow.shape[0], 2, PIXELS // (WIDTH * BLOCK), side)
    wide = jnp.repeat(jnp.repeat(grid, BLOCK, 2), BLOCK, 3)
    row = lax.broadcasted_iota(jnp.int32, wide.shape[2:], 0)
    col = lax.broadcasted_iota(jnp.int32, wide.shape[2:], 1)
    source_col = col + wide[:, 1]
    local_row = row % BLOCK + wide[:, 0] + REACH
    cell = jnp.where(
        (source_col >= 0) & (source_col < WIDTH), local_row * WIDTH + source_col, -1
    )
    return cell.reshape(flow.shape[0], PIXELS)


def on_device(
    features,
    flow_forward,
    flow_backward,
    w_forward_in,
    b_forward_in,
    w_forward_out,
    b_forward_out,
    w_backward_in,
    b_backward_in,
    w_backward_out,
    b_backward_out,
    w_merge,
    b_merge,
    w_head,
    b_head,
    target,
):
    clips = features.shape[0]
    sections = lax.axis_size("tm")
    group = lax.axis_size("clip")
    scale = 1.0 / (clips * group * sections)
    flows = jnp.concatenate([flow_forward[:, 0], flow_backward[:, 0]], axis=0)
    cells = window_cells(flows)
    anywhere = pl.BlockSpec(memory_space=pl.ANY)
    vmem = pl.BlockSpec(memory_space=pltpu.VMEM)
    dma = pltpu.SemaphoreType.DMA
    all_feats, all_cells = pl.pallas_call(
        functools.partial(gather_kernel, sections),
        out_shape=(
            jax.ShapeDtypeStruct((sections, clips, CHANNELS, PIXELS), BF),
            jax.ShapeDtypeStruct((sections, 2 * clips, PIXELS), jnp.int32),
        ),
        in_specs=[anywhere] * 2,
        out_specs=[anywhere] * 2,
        scratch_shapes=[dma((2,)), dma((2, sections)), dma((2, sections))],
        compiler_params=pltpu.CompilerParams(collective_id=0, has_side_effects=True),
        name="gather",
    )(features[:, 0], cells)
    column = lambda b: b[:, None]
    restored, pack = pl.pallas_call(
        functools.partial(compute_kernel, sections, scale),
        out_shape=(
            jax.ShapeDtypeStruct((clips, SUBPIX, PIXELS), BF),
            jax.ShapeDtypeStruct((PACK_ROWS, PACK_COLS), F32),
        ),
        in_specs=[vmem] * 15,
        out_specs=[vmem] * 2,
        scratch_shapes=[
            pltpu.VMEM((2, clips, CHANNELS, PIXELS + 2 * MARGIN), BF),
            pltpu.VMEM((2, 3 * CHANNELS, 6 * CHANNELS), BF),
            pltpu.VMEM((2, CHANNELS, 1), F32),
            pltpu.VMEM((2, 3 * CHANNELS, 3 * CHANNELS), BF),
            pltpu.VMEM((2, CHANNELS, 1), F32),
        ],
        compiler_params=pltpu.CompilerParams(vmem_limit_bytes=48 << 20),
        name="compute",
    )(
        all_feats,
        all_cells,
        w_forward_in,
        column(b_forward_in),
        w_forward_out,
        column(b_forward_out),
        w_backward_in,
        column(b_backward_in),
        w_backward_out,
        column(b_backward_out),
        w_merge,
        column(b_merge),
        w_head,
        column(b_head),
        target[:, 0],
    )
    rows = PACK_ROWS // group
    grad_merge, grad_head, loss = pl.pallas_call(
        functools.partial(reduce_kernel, group, sections),
        out_shape=(
            jax.ShapeDtypeStruct((CHANNELS, 18 * CHANNELS), F32),
            jax.ShapeDtypeStruct((SUBPIX, CHANNELS), F32),
            jax.ShapeDtypeStruct((1, 1), F32),
        ),
        in_specs=[vmem],
        out_specs=[vmem] * 3,
        scratch_shapes=[
            pltpu.VMEM((group, rows, PACK_COLS), F32),
            pltpu.VMEM((sections, rows, PACK_COLS), F32),
            pltpu.VMEM((PACK_ROWS, PACK_COLS), F32),
            dma((group,)),
            dma((group,)),
            dma((sections,)),
            dma((sections,)),
            dma((group,)),
            dma((group,)),
        ],
        compiler_params=pltpu.CompilerParams(collective_id=1, has_side_effects=True),
        name="reduce",
    )(pack)
    return (restored[:, None], grad_merge, grad_head, loss[0, 0])


def solution(mesh):
    split = P("clip", "tm", None, None)
    in_specs = (split,) * 3 + (P(),) * 12 + (split,)
    out_specs = (split, P(), P(), P())
    return jax.shard_map(
        on_device, mesh=mesh, in_specs=in_specs, out_specs=out_specs, check_vma=False
    )
```

time: 340 us -> 80.5 us (0.24)
  waiting for transfers between devices: 125 us -> 0 us
  matrix products: 94.5 us -> 0 us
  Pallas kernels: 0 us -> 65.3 us
  blocking collectives: 42.1 us -> 0 us
  starting transfers between devices: 28.9 us -> 0 us
  between operations: 15.5 us -> 2.62 us
  local copies, waits for them, and re-layouts: 23.4 us -> 11.4 us
  loops' own time: 4.8 us -> 0 us
  other arithmetic: 5.51 us -> 0.81 us
    dot_general x388 -> x0, matrix products: 94.5 us -> none  [the longest x306 74.1 us: apply_taps(): term = jnp.dot(block, group[tap_index], preferred_element_type=jnp.float32)]
    psum x1 -> x0, waiting for transfers between devices: 83.7 us -> none  [on_device(): lax.psum((totals[0], totals[1], totals[2]), ('clip', 'tm'))]
    pallas_call x0 -> x3, Pallas kernels: none -> 65.3 us  [the longest x1 25.9 us: on_device(): pl.pallas_call(functools.partial(reduce_kernel, group, sections), out_sha...]
    psum x1 -> x0, blocking collectives: 42.1 us -> none  [on_device(): lax.psum((totals[0], totals[1], totals[2]), ('clip', 'tm'))]
    ppermute x10 -> x0, waiting for transfers between devices: 40.9 us -> none  [shifted(): lax.ppermute(value, axis, [(source, source + steps) for source in range(f...]
    ppermute x10 -> x0, starting transfers between devices: 28.9 us -> none  [shifted(): lax.ppermute(value, axis, [(source, source + steps) for source in range(f...]
    unnamed x36 -> x40, local copies, waits for them, and re-layouts: 3.16 us -> 9.81 us
    broadcast_in_dim x92 -> x7, local copies, waits for them, and re-layouts: 6.95 us -> 0.65 us  [the longest x6 0.57 us: on_device(): column = lambda b: b[:, None]]
  transfers between devices with their start and end apart: 11 -> 0, of which waited for: 11 -> 0; matrix products, arithmetic and copies ran while one was open for 0% -> 0% of each run, Pallas kernels for 0% -> 0%
where the time goes in v1:
time: 80.5 us; the launch traced here: 80.1 us
  Pallas kernels  65.3 us (81%)
  local copies, waits for them, and re-layouts  11.4 us (14%)
  between operations  2.62 us (3%)
  other arithmetic  0.81 us (1%)
    pallas_call x1, Pallas kernels, on_device(): pl.pallas_call(functools.partial(reduce_kernel, group, sections), out_sha...  25.9 us
    pallas_call x1, Pallas kernels, on_device(): pl.pallas_call(functools.partial(gather_kernel, sections), out_shape=(jax...  24.9 us
    pallas_call x1, Pallas kernels, on_device(): pl.pallas_call(functools.partial(compute_kernel, sections, scale), out_sh...  14.5 us
    unnamed x40, local copies, waits for them, and re-layouts  9.81 us

profile of v1, /device:TPU:0, one launch (start us, length us, event | category | flops | bytes accessed | tf_op | source)
XLA Modules:
  0.0 80.1 jit_solution(14106784965760574567)
XLA Ops:
  0.7 0.0 copy-start.11
  0.7 0.7 copy-done.11
  1.3 0.0 copy-start.12
  1.3 0.1 concatenate.8
  1.4 0.6 copy-done.12
  2.0 0.1 concatenate.9
  2.1 0.1 copy.28
  2.2 0.2 fusion
  2.4 0.1 select_n.20
  2.5 0.0 copy-start.18
  2.5 0.1 add.38
  2.6 0.6 copy-done.18
  3.2 0.0 copy-start.13
  3.2 0.1 copy.36.bh
  3.3 0.6 copy-done.13
  3.8 0.0 copy-start.14
  3.8 0.1 copy.31.bfi
  3.9 0.6 copy-done.14
  4.5 0.0 copy-start.15
  4.5 0.1 copy.32.bfo
  4.6 0.6 copy-done.15
  5.1 0.0 copy-start.16
  5.1 0.1 copy.33.bbi
  5.2 0.6 copy-done.16
  5.8 0.0 copy-start.17
  5.8 0.1 copy.34.bbo
  5.9 0.6 copy-done.17
  6.4 0.1 copy.35.bm
  6.5 0.1 broadcast_in_dim.33
  6.6 0.1 reshape.55
  6.8 0.0 copy-start.7
  6.8 0.0 copy-start.5
  6.8 0.1 copy.29
  6.9 0.0 copy-start.6
  6.9 0.1 squeeze.18
  7.0 0.0 copy-start.4
  7.0 0.1 copy.30
  7.1 0.0 copy-start.2
  7.1 0.1 squeeze.19
  7.2 0.6 add_select_fusion.cell_ref
  7.8 0.0 copy-start.3
  7.8 0.0 copy-start.9
  7.8 24.9 %gather.1 = (bf16[4,2,64,1024]{3,2,1,0:T(8,128)(2,1)}, s32[4,4,1024]{2,1,0:T(4,128)}) custom-call(bf16[2,64,1024]{2,1,0:T(8,128)(2,1)} %bitcast.25, s32[4,1024]{1,0:T(4,128)} %add_select_fusion.cell_ref), custom_call_target="tpu_custom_call" | custom-call | tf_op jit(solution)/shard_map/gather/pallas_call | solution.py:365
  32.7 0.0 copy-done.7
  32.7 0.0 copy-done.5
  32.7 0.0 copy-done.6
  32.7 0.0 copy-done.4
  32.7 0.0 copy-done.2
  32.8 0.0 copy-done.3
  32.8 0.0 copy-done.9
  32.8 0.0 copy-start
  32.8 1.2 %copy-done = bf16[4,2,64,1024]{3,2,1,0:T(8,128)(2,1)S(1)} copy-done((bf16[4,2,64,1024]{3,2,1,0:T(8,128)(2,1)S(1)}, bf16[4,2,64,1024]{3,2,1,0:T(8,128)(2,1)}, u32[]{:S(2)}) %copy-start) | copy-done | bytes 1048600
  34.0 0.0 copy-start.8
  34.0 0.8 %copy-done.8 = s32[4,4,1024]{2,1,0:T(4,128)S(1)} copy-done((s32[4,4,1024]{2,1,0:T(4,128)S(1)}, s32[4,4,1024]{2,1,0:T(4,128)}, u32[]{:S(2)}) %copy-start.8) | copy-done | bytes 65560
  34.8 14.5 %compute.1 = (bf16[2,48,1024]{2,1,0:T(8,128)(2,1)}, f32[256,384]{1,0:T(8,128)S(1)}) custom-call(bf16[4,2,64,1024]{3,2,1,0:T(8,128)(2,1)S(1)} %copy-done, s32[4,4,1024]{2,1,0:T(4,128)S(1)} %copy-done.8, bf16[64,1152]{1,0:T(8,128)(2,1)S(1)} %copy-done.3, f32[64,1]{1,0:T(8,128)S(1)} %copy.31.bfi, bf16[64,576]{1,0:T(8,128)(2,1)S(1)} %copy-done.6, ...), custom_call_target="tpu_custom_call" | custom-call | tf_op jit(solution)/shard_map/compute/pallas_call | solution.py:378
  49.3 0.0 copy-start.1
  49.4 0.7 copy-done.1
  50.1 25.9 %reduce.5 = (f32[64,1152]{1,0:T(8,128)}, f32[48,64]{1,0:T(8,128)}, f32[1,1]{1,0:T(1,128)}) custom-call(f32[256,384]{1,0:T(8,128)} %copy-done.1), custom_call_target="tpu_custom_call" | custom-call | tf_op jit(solution)/shard_map/reduce/pallas_call | solution.py:413
  76.0 0.0 copy-start.10
  76.0 1.7 %copy.41 = f32[64,1152]{1,0:T(8,128)} copy(f32[64,1152]{1,0:T(8,128)} %get-tuple-element.35) | data formatting | bytes 589824
  77.7 0.0 copy-done.10
  77.7 0.6 copy.42
  (6 shorter events, 0.0 us)
Async XLA Ops:
  0.7 0.7 copy-start.11
  1.3 0.7 copy-start.12
  2.5 0.7 copy-start.18
  3.2 0.7 copy-start.13
  3.8 0.7 copy-start.14
  4.5 0.7 copy-start.15
  5.1 0.7 copy-start.16
  5.8 0.7 copy-start.17
  6.8 25.9 %copy-start.7 = (bf16[64,576]{1,0:T(8,128)(2,1)S(1)}, bf16[64,576]{1,0:T(8,128)(2,1)}, u32[]{:S(2)}) copy-start(bf16[64,576]{1,0:T(8,128)(2,1)} %wbo.1) | copy-start | bytes 221188
  6.8 25.9 %copy-start.5 = (bf16[64,1152]{1,0:T(8,128)(2,1)S(1)}, bf16[64,1152]{1,0:T(8,128)(2,1)}, u32[]{:S(2)}) copy-start(bf16[64,1152]{1,0:T(8,128)(2,1)} %wm.1) | copy-start | bytes 442372
  6.9 25.8 %copy-start.6 = (bf16[64,576]{1,0:T(8,128)(2,1)S(1)}, bf16[64,576]{1,0:T(8,128)(2,1)}, u32[]{:S(2)}) copy-start(bf16[64,576]{1,0:T(8,128)(2,1)} %wfo.1) | copy-start | bytes 221188
  7.0 25.7 %copy-start.4 = (bf16[64,1152]{1,0:T(8,128)(2,1)S(1)}, bf16[64,1152]{1,0:T(8,128)(2,1)}, u32[]{:S(2)}) copy-start(bf16[64,1152]{1,0:T(8,128)(2,1)} %wbi.1) | copy-start | bytes 442372
  7.1 25.6 %copy-start.2 = (bf16[2,1,48,1024]{3,2,1,0:T(8,128)(2,1)S(1)}, bf16[2,1,48,1024]{3,2,1,0:T(8,128)(2,1)}, u32[]{:S(2)}) copy-start(bf16[2,1,48,1024]{3,2,1,0:T(8,128)(2,1)} %param.31) | copy-start | bytes 589828
  7.8 24.9 %copy-start.3 = (bf16[64,1152]{1,0:T(8,128)(2,1)S(1)}, bf16[64,1152]{1,0:T(8,128)(2,1)}, u32[]{:S(2)}) copy-start(bf16[64,1152]{1,0:T(8,128)(2,1)} %wfi.1) | copy-start | bytes 442372
  7.8 24.9 %copy-start.9 = (bf16[48,64]{1,0:T(8,128)(2,1)S(1)}, bf16[48,64]{1,0:T(8,128)(2,1)}, u32[]{:S(2)}) copy-start(bf16[48,64]{1,0:T(8,128)(2,1)} %wh.1) | copy-start | bytes 18436
  32.8 1.2 %copy-start = (bf16[4,2,64,1024]{3,2,1,0:T(8,128)(2,1)S(1)}, bf16[4,2,64,1024]{3,2,1,0:T(8,128)(2,1)}, u32[]{:S(2)}) copy-start(bf16[4,2,64,1024]{3,2,1,0:T(8,128)(2,1)} %get-tuple-element.11.feat_ref) | copy-start | bytes 3145732
  34.0 0.8 %copy-start.8 = (s32[4,4,1024]{2,1,0:T(4,128)S(1)}, s32[4,4,1024]{2,1,0:T(4,128)}, u32[]{:S(2)}) copy-start(s32[4,4,1024]{2,1,0:T(4,128)} %get-tuple-element.12.cell_ref) | copy-start | bytes 196612
  49.3 0.8 copy-start.1
  76.0 1.7 %copy-start.10 = (f32[48,64]{1,0:T(8,128)S(1)}, f32[48,64]{1,0:T(8,128)}, u32[]{:S(2)}) copy-start(f32[48,64]{1,0:T(8,128)} %get-tuple-element.36) | copy-start | bytes 36868

commit v2 on v1

v2 whole, which is shorter than its diff:
```python
import functools

import jax
import jax.numpy as jnp
from jax import lax
from jax.experimental import pallas as pl
from jax.experimental.pallas import tpu as pltpu
from jax.sharding import PartitionSpec as P

CHANNELS = 64
SUBPIX = 48
WIDTH = 32
PIXELS = 1024
BLOCK = 8
REACH = 4
TILE = 256
MARGIN = REACH * WIDTH
WINDOW = TILE + 2 * MARGIN
CLIP_LIMIT = 128.0
LEAK = 0.1
PACK_ROWS = 256
PACK_COLS = 384
MESH = pl.DeviceIdType.MESH
BF = jnp.bfloat16
F32 = jnp.float32
PART_TYPE = F32


def roll_lanes(value, shift):
    return pltpu.roll(value, shift % PIXELS, 1)


def lane_masks():
    lane = lax.broadcasted_iota(jnp.int32, (1, PIXELS), 1)
    col = lane % WIDTH
    return (
        (col != 0),
        (col != WIDTH - 1),
        (lane >= WIDTH),
        (lane < PIXELS - WIDTH),
    )


def column_taps(value, masks):
    left = jnp.where(masks[0], roll_lanes(value, 1), 0.0)
    right = jnp.where(masks[1], roll_lanes(value, -1), 0.0)
    return [left.astype(BF), value.astype(BF), right.astype(BF)]


def row_sum(stacked, masks):
    up = jnp.where(masks[2], roll_lanes(stacked[:CHANNELS], WIDTH), 0.0)
    down = jnp.where(masks[3], roll_lanes(stacked[2 * CHANNELS :], -WIDTH), 0.0)
    return up + stacked[CHANNELS : 2 * CHANNELS] + down


def dot(a, b):
    return jnp.dot(a, b, preferred_element_type=F32)


def dot_t(a, b):
    return lax.dot_general(a, b, (((1,), (1,)), ((), ())), preferred_element_type=F32)


def stack_rows(weight):
    third = weight.shape[1] // 3
    return jnp.concatenate([weight[:, i * third : (i + 1) * third] for i in range(3)], axis=0)


def merge(hf, hb, target, w_merge, b_merge, w_head, b_head, scale, masks):
    taps_f = column_taps(hf.astype(F32), masks)
    taps_b = column_taps(hb.astype(F32), masks)
    joined = jnp.concatenate([t for pair in zip(taps_f, taps_b) for t in pair], axis=0)
    m = row_sum(dot(w_merge, joined), masks) + b_merge
    sig = jax.nn.sigmoid(m)
    active = (m * sig).astype(BF)
    out = dot(w_head, active) + b_head
    misfit = out - target.astype(F32)
    loss = jnp.sum(misfit * misfit, axis=0, keepdims=True)
    loss = jnp.sum(loss, axis=1, keepdims=True) * (0.5 * scale)
    err = (misfit * scale).astype(BF)
    g_head = dot_t(err, active)
    back = lax.dot_general(w_head, err, (((0,), (0,)), ((), ())), preferred_element_type=F32)
    d_m = (back * (sig * (1.0 + m * (1.0 - sig)))).astype(BF).astype(F32)
    above = jnp.where(masks[3], roll_lanes(d_m, -WIDTH), 0.0).astype(BF)
    below = jnp.where(masks[2], roll_lanes(d_m, WIDTH), 0.0).astype(BF)
    g_merge = dot_t(jnp.concatenate([above, d_m.astype(BF), below], axis=0), joined)
    return out.astype(BF), g_merge, g_head, loss


def window_cells(flow_ref, clip, start):
    lane = lax.broadcasted_iota(jnp.int32, (1, TILE), 1)
    row, col = lane // WIDTH, lane % WIDTH
    side = WIDTH // BLOCK
    first = start // TILE * side

    def offsets(part):
        value = jnp.full((1, TILE), flow_ref[clip, 0, part, first], jnp.int32)
        for b in range(1, side):
            value = jnp.where(col >= b * BLOCK, flow_ref[clip, 0, part, first + b], value)
        return value

    source_col = col + offsets(1)
    cell = (row + offsets(0) + REACH) * WIDTH + source_col
    return jnp.where((source_col >= 0) & (source_col < WIDTH), cell, -1)


def fused_kernel(group, sections, scale, *refs):
    n_in = 14
    flows = refs[:2]
    hbm_in = refs[2 : 2 + n_in]
    out_ref, gm_ref, gh_ref, loss_ref = refs[2 + n_in : 6 + n_in]
    held = refs[6 + n_in : 6 + 2 * n_in]
    (
        in_sem,
        out_buf,
        out_sem,
        w_g,
        w_x,
        w_out,
        b_in,
        b_out,
        one_hot,
        fixed,
        prior,
        state,
        hop_send,
        hop_recv,
        acc_gm,
        acc_gh,
        acc_loss,
        pack,
        got,
        part,
        full,
        send1,
        recv1,
        send2,
        recv2,
        send3,
        recv3,
    ) = refs[6 + 2 * n_in :]
    feat, wfi, bfi, wfo, bfo, wbi, bbi, wbo, bbo, wm, bm, wh, bh, target = held
    clips = feat.shape[0]
    rows = PACK_ROWS // group
    me = lax.axis_index("clip")
    sec = lax.axis_index("tm")

    loads = [
        pltpu.make_async_copy(a, b, in_sem.at[k]) for k, (a, b) in enumerate(zip(hbm_in, held))
    ]
    for load in loads:
        load.start()
    prior[...] = jnp.zeros_like(prior)
    barrier = pltpu.get_barrier_semaphore()
    for off in range(1, group):
        pl.semaphore_signal(
            barrier, 1, device_id={"clip": lax.rem(me + off, group)}, device_id_type=MESH
        )
    for off in range(1, sections):
        pl.semaphore_signal(
            barrier, 1, device_id={"tm": lax.rem(sec + off, sections)}, device_id_type=MESH
        )
    for load in loads:
        load.wait()

    masks = lane_masks()
    eye = lax.broadcasted_iota(jnp.int32, (CHANNELS, CHANNELS), 0) == lax.broadcasted_iota(
        jnp.int32, (CHANNELS, CHANNELS), 1
    )

    def column(row):
        n = row.shape[1]
        return jnp.sum(jnp.where(eye[:n, :n], row, 0.0), axis=1, keepdims=True)

    def part_rows(weight, first):
        return jnp.concatenate(
            [
                jnp.concatenate(
                    [
                        weight[:, (3 * dy + dx) * 128 + first : (3 * dy + dx) * 128 + first + 64]
                        for dx in range(3)
                    ],
                    axis=1,
                )
                for dy in range(3)
            ],
            axis=0,
        )

    for d, (wi, bi, wo, bo) in enumerate(((wfi, bfi, wfo, bfo), (wbi, bbi, wbo, bbo))):
        w_g[d] = part_rows(wi[...], 0)
        w_x[d] = part_rows(wi[...], CHANNELS)
        w_out[d] = stack_rows(wo[...])
        b_in[d] = column(bi[...])
        b_out[d] = column(bo[...])
    pl.semaphore_wait(barrier, group + sections - 2)

    window_cell = lax.broadcasted_iota(jnp.int32, (WINDOW, TILE), 0)
    inner = pl.ds(MARGIN, PIXELS)

    def hop(d, c):
        slot = d * clips + c
        return pltpu.make_async_remote_copy(
            state.at[d, c],
            prior.at[d, c, :, inner],
            hop_send.at[slot],
            hop_recv.at[slot],
            device_id={"tm": sec + 1 - 2 * d},
            device_id_type=MESH,
        )

    def place(d):
        return jnp.where(d == 0, sec, sections - 1 - sec)

    def step(d, c):
        for k, start in enumerate(range(0, PIXELS, TILE)):
            cells = jnp.where(
                d == 0, window_cells(flows[0], c, start), window_cells(flows[1], c, start)
            )
            one_hot[k] = (window_cell == cells).astype(F32).astype(BF)
        taps_x = jnp.concatenate(column_taps(feat[c, 0].astype(F32), masks), axis=0)
        fixed[...] = row_sum(dot(w_x[d], taps_x), masks) + b_in[d]

        @pl.when(place(d) > 0)
        def _():
            hop(d, c).wait_recv()

        warped = jnp.concatenate(
            [
                dot(prior[d, c, :, start : start + WINDOW], one_hot[start // TILE])
                for start in range(0, PIXELS, TILE)
            ],
            axis=1,
        )
        taps_g = jnp.concatenate(column_taps(warped, masks), axis=0)
        hidden = row_sum(dot(w_g[d], taps_g), masks) + fixed[...]
        hidden = jnp.where(hidden >= 0, hidden, LEAK * hidden).astype(BF).astype(F32)
        taps_a = jnp.concatenate(column_taps(hidden, masks), axis=0)
        update = row_sum(dot(w_out[d], taps_a), masks) + b_out[d]
        state[d, c] = (warped + update).astype(BF)

        @pl.when(place(d) < sections - 1)
        def _():
            hop(d, c).start()

    early = jnp.where(2 * sec < sections, 0, 1)

    def first_turn(c, carry):
        step(early, c)
        return carry

    lax.fori_loop(0, clips, first_turn, 0)
    acc_gm[...] = jnp.zeros_like(acc_gm)
    acc_gh[...] = jnp.zeros_like(acc_gh)
    acc_loss[...] = jnp.zeros_like(acc_loss)
    w_merge = stack_rows(wm[...])
    b_merge = column(bm[...])
    b_head = column(bh[...])

    def store_out(c):
        return pltpu.make_async_copy(out_buf.at[c], out_ref.at[c, 0], out_sem.at[c])

    def last_turn(c, carry):
        step(1 - early, c)
        out, g_merge, g_head, loss = merge(
            state[0, c],
            state[1, c],
            target[c, 0],
            w_merge,
            b_merge,
            wh[...],
            b_head,
            scale,
            masks,
        )
        out_buf[c] = out
        store_out(c).start()
        acc_gm[...] += g_merge
        acc_gh[...] += g_head
        acc_loss[...] += loss
        return carry

    lax.fori_loop(0, clips, last_turn, 0)

    top = 3 * CHANNELS
    g_merge = acc_gm[...]
    extra = jnp.concatenate(
        [
            jnp.concatenate(
                [acc_gh[...], jnp.zeros((SUBPIX, CHANNELS), F32)],
                axis=1,
            ),
            jnp.broadcast_to(acc_loss[...], (PACK_ROWS - top - SUBPIX, 128)),
        ],
        axis=0,
    )
    extra = jnp.concatenate(
        [extra, jnp.zeros((PACK_ROWS - top, PACK_COLS - 128), F32)], axis=1
    )
    packed = jnp.concatenate([g_merge, extra], axis=0)
    for g in range(group):
        pack[g] = packed[g * rows : (g + 1) * rows].astype(pack.dtype)

    copies = []
    for off in range(1, group):
        peer = lax.rem(me + off, group)
        copies.append(
            pltpu.make_async_remote_copy(
                pack.at[peer],
                got.at[off],
                send1.at[off],
                recv1.at[off],
                device_id={"clip": peer},
                device_id_type=MESH,
            )
        )
    for copy in copies:
        copy.start()
    total = pack[me].astype(F32)
    for off, copy in enumerate(copies, 1):
        copy.wait_recv()
        total = total + got[off].astype(F32)
    part[sec] = total.astype(part.dtype)
    more = []
    for off in range(1, sections):
        more.append(
            pltpu.make_async_remote_copy(
                part.at[sec],
                part.at[sec],
                send2.at[off],
                recv2.at[off],
                device_id={"tm": lax.rem(sec + off, sections)},
                device_id_type=MESH,
            )
        )
    for copy in more:
        copy.start()
    for copy in copies:
        copy.wait_send()
    for copy in more:
        copy.wait_recv()
    total = part[0].astype(F32)
    for s in range(1, sections):
        total = total + part[s].astype(F32)
    high = total.astype(full.dtype)
    low = (total - high.astype(F32))[:, :128]
    lane = lax.broadcasted_iota(jnp.int32, (rows, PACK_COLS), 1)
    row = lax.broadcasted_iota(jnp.int32, (rows, PACK_COLS), 0) + me * rows
    low = jnp.concatenate([low, low, low], axis=1)
    spare = (row >= top) & (lane >= 256)
    full[me] = jnp.where(spare, low, high.astype(F32)).astype(full.dtype)
    last = []
    for off in range(1, group):
        last.append(
            pltpu.make_async_remote_copy(
                full.at[me],
                full.at[me],
                send3.at[off],
                recv3.at[off],
                device_id={"clip": lax.rem(me + off, group)},
                device_id_type=MESH,
            )
        )
    for copy in last:
        copy.start()
    for copy in more:
        copy.wait_send()
    for c in range(clips):
        store_out(c).wait()
    for d in range(2):

        @pl.when(place(d) < sections - 1)
        def _():
            for c in range(clips):
                hop(d, c).wait_send()

    for copy in last:
        copy.wait()
    summed = jnp.concatenate([full[g].astype(F32) for g in range(group)], axis=0)
    g_merge = summed[:top]
    g_head = summed[top : top + SUBPIX, :CHANNELS]

    def squares(v):
        return jnp.sum(jnp.sum(v * v, axis=0, keepdims=True), axis=1, keepdims=True)

    factor = jnp.minimum(1.0, CLIP_LIMIT / jnp.sqrt(squares(g_merge) + squares(g_head) + 1e-06))
    for i in range(3):
        gm_ref[:, i * PACK_COLS : (i + 1) * PACK_COLS] = (
            g_merge[i * CHANNELS : (i + 1) * CHANNELS] * factor
        )
    gh_ref[...] = g_head * factor
    end = top + SUBPIX
    loss_ref[...] = summed[end : end + 1, 0:1] + summed[end : end + 1, 256:257]


def on_device(features, flow_forward, flow_backward, *rest):
    weights, target = list(rest[:-1]), rest[-1]
    clips = features.shape[0]
    sections = lax.axis_size("tm")
    group = lax.axis_size("clip")
    scale = 1.0 / (clips * group * sections)
    held = [features, *(w[None] if w.ndim == 1 else w for w in weights), target]
    anywhere = pl.BlockSpec(memory_space=pl.ANY)
    vmem = pl.BlockSpec(memory_space=pltpu.VMEM)
    smem = pl.BlockSpec(memory_space=pltpu.SMEM)
    dma = pltpu.SemaphoreType.DMA
    rows = PACK_ROWS // group
    third = 3 * CHANNELS
    restored, grad_merge, grad_head, loss = pl.pallas_call(
        functools.partial(fused_kernel, group, sections, scale),
        out_shape=(
            jax.ShapeDtypeStruct((clips, 1, SUBPIX, PIXELS), BF),
            jax.ShapeDtypeStruct((CHANNELS, 18 * CHANNELS), F32),
            jax.ShapeDtypeStruct((SUBPIX, CHANNELS), F32),
            jax.ShapeDtypeStruct((1, 1), F32),
        ),
        in_specs=[smem] * 2 + [anywhere] * len(held),
        out_specs=[anywhere] + [vmem] * 3,
        scratch_shapes=[pltpu.VMEM(a.shape, a.dtype) for a in held]
        + [
            dma((len(held),)),
            pltpu.VMEM((clips, SUBPIX, PIXELS), BF),
            dma((clips,)),
            pltpu.VMEM((2, third, third), BF),
            pltpu.VMEM((2, third, third), BF),
            pltpu.VMEM((2, third, third), BF),
            pltpu.VMEM((2, CHANNELS, 1), F32),
            pltpu.VMEM((2, CHANNELS, 1), F32),
            pltpu.VMEM((PIXELS // TILE, WINDOW, TILE), BF),
            pltpu.VMEM((CHANNELS, PIXELS), F32),
            pltpu.VMEM((2, clips, CHANNELS, PIXELS + 2 * MARGIN), BF),
            pltpu.VMEM((2, clips, CHANNELS, PIXELS), BF),
            dma((2 * clips,)),
            dma((2 * clips,)),
            pltpu.VMEM((third, 6 * CHANNELS), F32),
            pltpu.VMEM((SUBPIX, CHANNELS), F32),
            pltpu.VMEM((1, 1), F32),
            pltpu.VMEM((group, rows, PACK_COLS), PART_TYPE),
            pltpu.VMEM((group, rows, PACK_COLS), PART_TYPE),
            pltpu.VMEM((sections, rows, PACK_COLS), PART_TYPE),
            pltpu.VMEM((group, rows, PACK_COLS), BF),
            dma((group,)),
            dma((group,)),
            dma((sections,)),
            dma((sections,)),
            dma((group,)),
            dma((group,)),
        ],
        compiler_params=pltpu.CompilerParams(
            collective_id=0, has_side_effects=True, vmem_limit_bytes=48 << 20
        ),
        name="step",
    )(flow_forward, flow_backward, *held)
    return (restored, grad_merge, grad_head, loss[0, 0])


def solution(mesh):
    split = P("clip", "tm", None, None)
    in_specs = (split,) * 3 + (P(),) * 12 + (split,)
    out_specs = (split, P(), P(), P())
    return jax.shard_map(
        on_device, mesh=mesh, in_specs=in_specs, out_specs=out_specs, check_vma=False
    )
```

time: 80.5 us -> 58.5 us (0.73)
  Pallas kernels: 65.3 us -> 45.8 us
  local copies, waits for them, and re-layouts: 11.4 us -> 9.78 us
  other arithmetic: 0.81 us -> 0 us
    pallas_call x3 -> x1, Pallas kernels: 65.3 us -> 45.8 us  [on_device(): pl.pallas_call(functools.partial(fused_kernel, group, sections, scale), o...]
    unnamed x40 -> x35, local copies, waits for them, and re-layouts: 9.81 us -> 9.78 us
where the time goes in v2:
time: 58.5 us; the launch traced here: 58.1 us
  Pallas kernels  45.8 us (78%)
  local copies, waits for them, and re-layouts  9.78 us (17%)
  between operations  2.49 us (4%)
    pallas_call x1, Pallas kernels, on_device(): pl.pallas_call(functools.partial(fused_kernel, group, sections, scale), o...  45.8 us
    unnamed x35, local copies, waits for them, and re-layouts  9.78 us

profile of v2, /device:TPU:0, one launch (start us, length us, event | category | flops | bytes accessed | tf_op | source)
XLA Modules:
  0.0 58.1 jit_solution(12486006220195844168)
XLA Ops:
  0.6 0.0 copy-start.13
  0.6 0.0 copy-start.14
  0.7 0.0 copy-start.15
  0.7 0.0 copy-start.9
  0.7 0.0 copy-start.8
  0.7 0.0 copy-start.10
  0.7 0.0 copy-start.11
  0.7 0.0 copy-start.12
  0.7 0.6 copy-done.13
  1.3 0.0 copy-done.14
  1.3 0.0 copy-done.15
  1.3 0.0 copy-done.9
  1.4 0.0 copy-done.8
  1.4 0.0 copy-done.10
  1.4 0.0 copy-done.11
  1.4 0.0 copy-done.12
  1.4 0.0 copy-start
  1.4 0.9 %copy-done = bf16[2,1,64,1024]{3,2,1,0:T(8,128)(2,1)S(1)} copy-done((bf16[2,1,64,1024]{3,2,1,0:T(8,128)(2,1)S(1)}, bf16[2,1,64,1024]{3,2,1,0:T(8,128)(2,1)}, u32[]{:S(2)}) %copy-start) | copy-done | bytes 262168
  2.4 0.0 copy-start.1
  2.4 0.9 %copy-done.1 = bf16[2,1,48,1024]{3,2,1,0:T(8,128)(2,1)S(1)} copy-done((bf16[2,1,48,1024]{3,2,1,0:T(8,128)(2,1)S(1)}, bf16[2,1,48,1024]{3,2,1,0:T(8,128)(2,1)}, u32[]{:S(2)}) %copy-start.1) | copy-done | bytes 196632
  3.3 0.0 copy-start.2
  3.3 0.9 %copy-done.2 = bf16[64,1152]{1,0:T(8,128)(2,1)S(1)} copy-done((bf16[64,1152]{1,0:T(8,128)(2,1)S(1)}, bf16[64,1152]{1,0:T(8,128)(2,1)}, u32[]{:S(2)}) %copy-start.2) | copy-done | bytes 147480
  4.2 0.0 copy-start.3
  4.2 0.9 %copy-done.3 = bf16[64,1152]{1,0:T(8,128)(2,1)S(1)} copy-done((bf16[64,1152]{1,0:T(8,128)(2,1)S(1)}, bf16[64,1152]{1,0:T(8,128)(2,1)}, u32[]{:S(2)}) %copy-start.3) | copy-done | bytes 147480
  5.1 0.0 copy-start.4
  5.1 0.9 %copy-done.4 = bf16[64,1152]{1,0:T(8,128)(2,1)S(1)} copy-done((bf16[64,1152]{1,0:T(8,128)(2,1)S(1)}, bf16[64,1152]{1,0:T(8,128)(2,1)}, u32[]{:S(2)}) %copy-start.4) | copy-done | bytes 147480
  6.0 0.0 copy-start.5
  6.0 0.9 %copy-done.5 = bf16[64,576]{1,0:T(8,128)(2,1)S(1)} copy-done((bf16[64,576]{1,0:T(8,128)(2,1)S(1)}, bf16[64,576]{1,0:T(8,128)(2,1)}, u32[]{:S(2)}) %copy-start.5) | copy-done | bytes 73752
  6.9 0.0 copy-start.6
  6.9 0.9 %copy-done.6 = bf16[64,576]{1,0:T(8,128)(2,1)S(1)} copy-done((bf16[64,576]{1,0:T(8,128)(2,1)S(1)}, bf16[64,576]{1,0:T(8,128)(2,1)}, u32[]{:S(2)}) %copy-start.6) | copy-done | bytes 73752
  7.8 0.0 copy-start.7
  7.8 0.7 %copy-done.7 = bf16[48,64]{1,0:T(8,128)(2,1)S(1)} copy-done((bf16[48,64]{1,0:T(8,128)(2,1)S(1)}, bf16[48,64]{1,0:T(8,128)(2,1)}, u32[]{:S(2)}) %copy-start.7) | copy-done | bytes 6168
  8.5 45.8 %step.1 = (bf16[2,1,48,1024]{3,2,1,0:T(8,128)(2,1)S(1)}, f32[64,1152]{1,0:T(8,128)S(1)}, f32[48,64]{1,0:T(8,128)S(1)}, f32[1,1]{1,0:T(1,128)}) custom-call(s32[2,1,2,16]{3,2,1,0:T(2,128)S(1)} %copy-done.8, s32[2,1,2,16]{3,2,1,0:T(2,128)S(1)} %copy-done.9, bf16[2,1,64,1024]{3,2,1,0:T(8,128)(2,1)S(1)} %copy-done, bf16[64,1152]{1,0:T(8,128)(2,1)S(1)} %copy-done.2, ...), custom_call_target="tpu_custom_call" | custom-call | tf_op jit(solution)/shard_map/step/pallas_call | solution.py:409
  54.3 0.7 %copy.24 = bf16[2,1,48,1024]{3,2,1,0:T(8,128)(2,1)} copy(bf16[2,1,48,1024]{3,2,1,0:T(8,128)(2,1)S(1)} %get-tuple-element.16) | data formatting | bytes 393216
  55.0 0.7 %copy.25 = f32[64,1152]{1,0:T(8,128)} copy(f32[64,1152]{1,0:T(8,128)S(1)} %get-tuple-element.17) | data formatting | bytes 589824
  55.7 0.6 %copy.26 = f32[48,64]{1,0:T(8,128)} copy(f32[48,64]{1,0:T(8,128)S(1)} %get-tuple-element.18) | data formatting | bytes 24576
Async XLA Ops:
  0.6 0.7 %copy-start.13 = (f32[64]{0:T(128)S(1)}, f32[64]{0:T(128)}, u32[]{:S(2)}) copy-start(f32[64]{0:T(128)} %param.26) | copy-start | bytes 772
  0.6 0.7 %copy-start.14 = (f32[64]{0:T(128)S(1)}, f32[64]{0:T(128)}, u32[]{:S(2)}) copy-start(f32[64]{0:T(128)} %param.28) | copy-start | bytes 772
  0.7 0.7 %copy-start.15 = (f32[48]{0:T(128)S(1)}, f32[48]{0:T(128)}, u32[]{:S(2)}) copy-start(f32[48]{0:T(128)} %param.30) | copy-start | bytes 580
  0.7 0.7 %copy-start.9 = (s32[2,1,2,16]{3,2,1,0:T(2,128)S(1)}, s32[2,1,2,16]{3,2,1,0:T(2,128)}, u32[]{:S(2)}) copy-start(s32[2,1,2,16]{3,2,1,0:T(2,128)} %refs_1_.1) | copy-start | bytes 772
  0.7 0.7 %copy-start.8 = (s32[2,1,2,16]{3,2,1,0:T(2,128)S(1)}, s32[2,1,2,16]{3,2,1,0:T(2,128)}, u32[]{:S(2)}) copy-start(s32[2,1,2,16]{3,2,1,0:T(2,128)} %refs_0_.1) | copy-start | bytes 772
  0.7 0.7 %copy-start.10 = (f32[64]{0:T(128)S(1)}, f32[64]{0:T(128)}, u32[]{:S(2)}) copy-start(f32[64]{0:T(128)} %param.20) | copy-start | bytes 772
  0.7 0.7 %copy-start.11 = (f32[64]{0:T(128)S(1)}, f32[64]{0:T(128)}, u32[]{:S(2)}) copy-start(f32[64]{0:T(128)} %param.22) | copy-start | bytes 772
  0.7 0.7 %copy-start.12 = (f32[64]{0:T(128)S(1)}, f32[64]{0:T(128)}, u32[]{:S(2)}) copy-start(f32[64]{0:T(128)} %param.24) | copy-start | bytes 772
  1.4 0.9 %copy-start = (bf16[2,1,64,1024]{3,2,1,0:T(8,128)(2,1)S(1)}, bf16[2,1,64,1024]{3,2,1,0:T(8,128)(2,1)}, u32[]{:S(2)}) copy-start(bf16[2,1,64,1024]{3,2,1,0:T(8,128)(2,1)} %refs_2_.1) | copy-start | bytes 786436
  2.4 0.9 %copy-start.1 = (bf16[2,1,48,1024]{3,2,1,0:T(8,128)(2,1)S(1)}, bf16[2,1,48,1024]{3,2,1,0:T(8,128)(2,1)}, u32[]{:S(2)}) copy-start(bf16[2,1,48,1024]{3,2,1,0:T(8,128)(2,1)} %refs_15_.1) | copy-start | bytes 589828
  3.3 0.9 %copy-start.2 = (bf16[64,1152]{1,0:T(8,128)(2,1)S(1)}, bf16[64,1152]{1,0:T(8,128)(2,1)}, u32[]{:S(2)}) copy-start(bf16[64,1152]{1,0:T(8,128)(2,1)} %refs_3_.1) | copy-start | bytes 442372
  4.2 0.9 %copy-start.3 = (bf16[64,1152]{1,0:T(8,128)(2,1)S(1)}, bf16[64,1152]{1,0:T(8,128)(2,1)}, u32[]{:S(2)}) copy-start(bf16[64,1152]{1,0:T(8,128)(2,1)} %refs_7_.1) | copy-start | bytes 442372
  5.1 0.9 %copy-start.4 = (bf16[64,1152]{1,0:T(8,128)(2,1)S(1)}, bf16[64,1152]{1,0:T(8,128)(2,1)}, u32[]{:S(2)}) copy-start(bf16[64,1152]{1,0:T(8,128)(2,1)} %refs_11_.1) | copy-start | bytes 442372
  6.0 0.9 %copy-start.5 = (bf16[64,576]{1,0:T(8,128)(2,1)S(1)}, bf16[64,576]{1,0:T(8,128)(2,1)}, u32[]{:S(2)}) copy-start(bf16[64,576]{1,0:T(8,128)(2,1)} %refs_5_.1) | copy-start | bytes 221188
  6.9 0.9 %copy-start.6 = (bf16[64,576]{1,0:T(8,128)(2,1)S(1)}, bf16[64,576]{1,0:T(8,128)(2,1)}, u32[]{:S(2)}) copy-start(bf16[64,576]{1,0:T(8,128)(2,1)} %refs_9_.1) | copy-start | bytes 221188
  7.8 0.7 %copy-start.7 = (bf16[48,64]{1,0:T(8,128)(2,1)S(1)}, bf16[48,64]{1,0:T(8,128)(2,1)}, u32[]{:S(2)}) copy-start(bf16[48,64]{1,0:T(8,128)(2,1)} %refs_13_.1) | copy-start | bytes 18436

commit v3 on v2

--- a/solution.py
+++ b/solution.py
@@ -400,7 +400,7 @@
     group = lax.axis_size("clip")
     scale = 1.0 / (clips * group * sections)
     held = [features, *(w[None] if w.ndim == 1 else w for w in weights), target]
-    anywhere = pl.BlockSpec(memory_space=pl.ANY)
+    anywhere = pl.BlockSpec(memory_space=pltpu.HBM)
     vmem = pl.BlockSpec(memory_space=pltpu.VMEM)
     smem = pl.BlockSpec(memory_space=pltpu.SMEM)
     dma = pltpu.SemaphoreType.DMA
@@ -447,7 +447,7 @@
             dma((group,)),
         ],
         compiler_params=pltpu.CompilerParams(
-            collective_id=0, has_side_effects=True, vmem_limit_bytes=48 << 20
+            collective_id=0, has_side_effects=True, vmem_limit_bytes=63 << 20
         ),
         name="step",
     )(flow_forward, flow_backward, *held)

time: 58.5 us -> 50.4 us (0.86)
  local copies, waits for them, and re-layouts: 9.78 us -> 3.01 us
  Pallas kernels: 45.8 us -> 44.7 us
    unnamed x35 -> x7, local copies, waits for them, and re-layouts: 9.78 us -> 3.01 us
    pallas_call x1, Pallas kernels: 45.8 us -> 44.7 us  [on_device(): pl.pallas_call(functools.partial(fused_kernel, group, sections, scale), o...]
where the time goes in v3:
time: 50.4 us; the launch traced here: 50.1 us
  Pallas kernels  44.7 us (89%)
  local copies, waits for them, and re-layouts  3.01 us (6%)
  between operations  2.39 us (5%)
    pallas_call x1, Pallas kernels, on_device(): pl.pallas_call(functools.partial(fused_kernel, group, sections, scale), o...  44.7 us
    unnamed x7, local copies, waits for them, and re-layouts  3.01 us

profile of v3, /device:TPU:0, one launch (start us, length us, event | category | flops | bytes accessed | tf_op | source)
XLA Modules:
  0.0 50.1 jit_solution(3110319966310911917)
XLA Ops:
  0.6 44.7 %step.1 = (bf16[2,1,48,1024]{3,2,1,0:T(8,128)(2,1)}, f32[64,1152]{1,0:T(8,128)}, f32[48,64]{1,0:T(8,128)}, f32[1,1]{1,0:T(1,128)}) custom-call(s32[2,1,2,16]{3,2,1,0:T(2,128)} %refs_0_.1, s32[2,1,2,16]{3,2,1,0:T(2,128)} %refs_1_.1, bf16[2,1,64,1024]{3,2,1,0:T(8,128)(2,1)} %refs_2_.1, bf16[64,1152]{1,0:T(8,128)(2,1)} %refs_3_.1, f32[1,64]{1,0:T(1,128)} %bitcast.7, ...), custom_call_target="tpu_custom_call" | custom-call | tf_op jit(solution)/shard_map/step/pallas_call | solution.py:409
  45.3 0.0 copy-start
  45.3 1.7 %copy.24 = bf16[2,1,48,1024]{3,2,1,0:T(8,128)(2,1)} copy(bf16[2,1,48,1024]{3,2,1,0:T(8,128)(2,1)} %get-tuple-element.16) | data formatting | bytes 393216
  47.0 0.0 copy-done
  47.0 0.0 copy-start.1
  47.0 0.7 %copy.25 = f32[64,1152]{1,0:T(8,128)} copy(f32[64,1152]{1,0:T(8,128)S(1)} %copy-done) | data formatting | bytes 589824
  47.7 0.0 copy-done.1
  47.7 0.6 %copy.26 = f32[48,64]{1,0:T(8,128)} copy(f32[48,64]{1,0:T(8,128)S(1)} %copy-done.1) | data formatting | bytes 24576
Async XLA Ops:
  45.3 1.7 %copy-start = (f32[64,1152]{1,0:T(8,128)S(1)}, f32[64,1152]{1,0:T(8,128)}, u32[]{:S(2)}) copy-start(f32[64,1152]{1,0:T(8,128)} %get-tuple-element.17) | copy-start | bytes 884740
  47.0 0.7 %copy-start.1 = (f32[48,64]{1,0:T(8,128)S(1)}, f32[48,64]{1,0:T(8,128)}, u32[]{:S(2)}) copy-start(f32[48,64]{1,0:T(8,128)} %get-tuple-element.18) | copy-start | bytes 36868

commit v4 on v3

--- a/solution.py
+++ b/solution.py
@@ -23,7 +23,7 @@
 MESH = pl.DeviceIdType.MESH
 BF = jnp.bfloat16
 F32 = jnp.float32
-PART_TYPE = F32
+PART_TYPE = BF
 
 
 def roll_lanes(value, shift):
@@ -391,6 +391,21 @@
     gh_ref[...] = g_head * factor
     end = top + SUBPIX
     loss_ref[...] = summed[end : end + 1, 0:1] + summed[end : end + 1, 256:257]
+
+
+def finish_kernel(*refs):
+    n = (len(refs) - 2) // 3
+    in_sem, out_sem = refs[-2:]
+    held = refs[2 * n : 3 * n]
+    loads = [pltpu.make_async_copy(refs[k], held[k], in_sem.at[k]) for k in range(n)]
+    stores = [pltpu.make_async_copy(held[k], refs[n + k], out_sem.at[k]) for k in range(n)]
+    for load in loads:
+        load.start()
+    for load, store in zip(loads, stores):
+        load.wait()
+        store.start()
+    for store in stores:
+        store.wait()
 
 
 def on_device(features, flow_forward, flow_backward, *rest):
@@ -451,6 +466,16 @@
         ),
         name="step",
     )(flow_forward, flow_backward, *held)
+    made = (restored, grad_merge, grad_head, loss)
+    restored, grad_merge, grad_head, loss = pl.pallas_call(
+        finish_kernel,
+        out_shape=tuple(jax.ShapeDtypeStruct(a.shape, a.dtype) for a in made),
+        in_specs=[anywhere] * 4,
+        out_specs=[anywhere] * 4,
+        scratch_shapes=[pltpu.VMEM(a.shape, a.dtype) for a in made] + [dma((4,)), dma((4,))],
+        compiler_params=pltpu.CompilerParams(vmem_limit_bytes=63 << 20),
+        name="finish",
+    )(*made)
     return (restored, grad_merge, grad_head, loss[0, 0])
 
 

time: 50.4 us -> 46.6 us (0.925)
  local copies, waits for them, and re-layouts: 3.01 us -> 0 us
  between operations: 2.39 us -> 0.65 us
  Pallas kernels: 44.7 us -> 45.7 us
    unnamed x7 -> x0, local copies, waits for them, and re-layouts: 3.01 us -> none
    pallas_call x0 -> x1, Pallas kernels: none -> 2.49 us  [on_device(): pl.pallas_call(finish_kernel, out_shape=tuple((jax.ShapeDtypeStruct(a.sha...]
    pallas_call x1, Pallas kernels: 44.7 us -> 43.3 us  [on_device(): pl.pallas_call(functools.partial(fused_kernel, group, sections, scale), o...]
where the time goes in v4:
time: 46.6 us; the launch traced here: 46.4 us
  Pallas kernels  45.7 us (98%)
  between operations  0.65 us (1%)
    pallas_call x1, Pallas kernels, on_device(): pl.pallas_call(functools.partial(fused_kernel, group, sections, scale), o...  43.3 us
    pallas_call x1, Pallas kernels, on_device(): pl.pallas_call(finish_kernel, out_shape=tuple((jax.ShapeDtypeStruct(a.sha...  2.49 us

profile of v4, /device:TPU:0, one launch (start us, length us, event | category | flops | bytes accessed | tf_op | source)
XLA Modules:
  0.0 46.4 jit_solution(10786744160279071792)
XLA Ops:
  0.6 43.3 %step.1 = (bf16[2,1,48,1024]{3,2,1,0:T(8,128)(2,1)}, f32[64,1152]{1,0:T(8,128)}, f32[48,64]{1,0:T(8,128)}, f32[1,1]{1,0:T(1,128)}) custom-call(s32[2,1,2,16]{3,2,1,0:T(2,128)} %refs_0_.1, s32[2,1,2,16]{3,2,1,0:T(2,128)} %refs_1_.1, bf16[2,1,64,1024]{3,2,1,0:T(8,128)(2,1)} %refs_2_.1, bf16[64,1152]{1,0:T(8,128)(2,1)} %refs_3_.1, f32[1,64]{1,0:T(1,128)} %bitcast.7, ...), custom_call_target="tpu_custom_call" | custom-call | tf_op jit(solution)/shard_map/step/pallas_call | solution.py:424
  43.9 2.5 %finish.1 = (bf16[2,1,48,1024]{3,2,1,0:T(8,128)(2,1)}, f32[64,1152]{1,0:T(8,128)}, f32[48,64]{1,0:T(8,128)}, f32[1,1]{1,0:T(1,128)}) custom-call(bf16[2,1,48,1024]{3,2,1,0:T(8,128)(2,1)} %get-tuple-element.12.refs_0_, f32[64,1152]{1,0:T(8,128)} %get-tuple-element.13.refs_1_, f32[48,64]{1,0:T(8,128)} %get-tuple-element.14.refs_2_, ...), custom_call_target="tpu_custom_call" | custom-call | tf_op jit(solution)/shard_map/finish/pallas_call | solution.py:470
